TPU v7x, 128 devices: a whole 4x4x4 slice. The times are simulated.
128 devices in a mesh: leaf: 4 (over y_hi, core), front: 32 (over y_lo, z, x).
Axes of the slice: x: 4, y: 4 (y_hi: 2, y_lo: 2; y = y_hi * 2 + y_lo), z: 4, core: 2. Of those that a mesh axis runs over, the one named last changes fastest.
Arguments:
- leaf_source: float32 [4, 2048, 128], P('leaf', 'front'), may hold values from -6 to 6
- mid_source: float32 [4, 2048, 128], P('leaf', 'front'), may hold values from -6 to 6
- root_source: float32 [8192, 128], P('front'), may hold values from -6 to 6
- leaf_inverse: float32 [4, 2, 2048, 2048], P('leaf', None, 'front'), may hold values from -0.09375 to 0.09375
- leaf_coupling: float32 [4, 2, 4096, 2048], P('leaf', None, None, 'front'), may hold values from -0.09375 to 0.09375
- mid_inverse: float32 [4, 2, 2048, 4096], P('leaf', None, None, 'front'), may hold values from -0.0625 to 0.0625
- mid_coupling: float32 [4, 2, 8192, 2048], P('leaf', None, None, 'front'), may hold values from -0.0625 to 0.0625
- root_inverse: float32 [2, 8192, 8192], P(None, 'leaf', 'front'), may hold values from -0.046875 to 0.046875
- leaf_blocks: int32 [4, 32], P('leaf'), may hold values from 0 to 31, as said below
- mid_blocks: int32 [2, 64], replicated, may hold values from 0 to 63, as said below
Outputs:
- leaf_solution: float32 [4, 2048, 128], P('leaf', 'front')
- mid_solution: float32 [4, 2048, 128], P('leaf', 'front')
- root_solution: float32 [8192, 128], P('front')
Inputs may be any that keep to these rules, and one draw needn't show every extreme that they name: `leaf_blocks`: each row holds every block number of a level-1 separator exactly once. `mid_blocks`: each row holds every block number of the root separator exactly once.
All inputs are finite; a program needn't handle non-finite values.
Results may differ from a plain program's by a relative error of at most 0.00015.
Values sent between devices are 32-bit elements; how exact they have to be, the bound alone decides.
A program may use at most 128 MiB of HBM per device.

v0:
```python
import jax
import jax.numpy as jnp
from jax import lax
from jax.sharding import PartitionSpec as P

exact_precision = lax.Precision.HIGHEST


def partner(value, axis, apart):
    return lax.ppermute(value, axis, [(i, i ^ 1 << apart) for i in range(lax.axis_size(axis))])


def complex_apply(matrix, vectors):
    width = vectors.shape[1] // 2
    real_part = jnp.dot(
        matrix[0], vectors, precision=exact_precision, preferred_element_type=jnp.float32
    )
    imag_part = jnp.dot(
        matrix[1], vectors, precision=exact_precision, preferred_element_type=jnp.float32
    )
    return jnp.concatenate(
        [real_part[:, :width] - imag_part[:, width:], real_part[:, width:] + imag_part[:, :width]],
        axis=1,
    )


def complex_transposed(matrix, vectors):
    width = vectors.shape[1] // 2
    dims = (((0,), (0,)), ((), ()))
    real_part = lax.dot_general(
        matrix[0], vectors, dims, precision=exact_precision, preferred_element_type=jnp.float32
    )
    imag_part = lax.dot_general(
        matrix[1], vectors, dims, precision=exact_precision, preferred_element_type=jnp.float32
    )
    return jnp.concatenate(
        [real_part[:, :width] - imag_part[:, width:], real_part[:, width:] + imag_part[:, :width]],
        axis=1,
    )


def pick_rows(matrix, block_order, row_count):
    positions = jnp.arange(row_count, dtype=jnp.int32)
    sources = jnp.take(block_order, positions // 128) * 128 + positions % 128
    return jnp.take(matrix, sources, axis=1)


def gather_rows(local_rows, update, initial):
    return update(initial, lax.all_gather(local_rows, "front", axis=0, tiled=True), jnp.int32(0))


def scatter_rows(term, rows_each):
    return lax.psum_scatter(
        term(jnp.int32(0), rows_each * lax.axis_size("front")),
        "front",
        scatter_dimension=0,
        tiled=True,
    )


def pair_swap(values):
    return partner(values, "leaf", 0)


def group_total(values):
    return lax.psum(values, "leaf")


def body(
    leaf_source,
    mid_source,
    root_source,
    leaf_inverse,
    leaf_coupling,
    mid_inverse,
    mid_coupling,
    root_inverse,
    leaf_blocks,
    mid_blocks,
):
    front_count = lax.axis_size("front")
    group = lax.axis_index("leaf")
    side = group % 2
    source_two = leaf_source[0]
    inverse_two = leaf_inverse[0]
    coupling_two = leaf_coupling[0]
    inverse_one = mid_inverse[0]
    coupling_one = mid_coupling[0]
    order_two = jnp.argsort(leaf_blocks[0])
    order_one = jnp.argsort(lax.dynamic_index_in_dim(mid_blocks, group // 2, 0, keepdims=False))
    width2 = source_two.shape[1]
    rows_two = source_two.shape[0]
    half_rows = mid_source.shape[1]
    block_rows = coupling_two.shape[1] // front_count
    root_block = root_source.shape[0]

    def fold_inverse_two(carry, shard_piece, row_start):
        return complex_apply(inverse_two, shard_piece)

    solved_two = gather_rows(source_two, fold_inverse_two, jnp.zeros(source_two.shape, jnp.float32))

    def lift_two(row_start, row_count):
        return complex_apply(pick_rows(coupling_two, order_two, row_count), solved_two)

    lifted = scatter_rows(lift_two, block_rows)
    placed = lax.dynamic_update_slice_in_dim(
        jnp.zeros((block_rows, width2), jnp.float32), mid_source[0], side * half_rows, 0
    )
    own_part = placed - lifted
    reduced_one = own_part + pair_swap(own_part)

    def apply_one(row_start, row_count):
        return complex_apply(inverse_one, reduced_one)

    solved_one = scatter_rows(apply_one, half_rows)

    def lift_one(row_start, row_count):
        return complex_apply(pick_rows(coupling_one, order_one, row_count), solved_one)

    gathered_terms = group_total(scatter_rows(lift_one, root_block))
    reduced_root = root_source - gathered_terms

    def apply_root(row_start, row_count):
        return complex_apply(root_inverse, reduced_root)

    solved_root = scatter_rows(apply_root, root_inverse.shape[1] // front_count)

    def fold_root(carry, shard_piece, row_start):
        return complex_transposed(root_inverse, shard_piece)

    partial_root = gather_rows(solved_root, fold_root, jnp.zeros(root_source.shape, jnp.float32))
    root_solution = group_total(partial_root)

    def fold_mid(carry, shard_piece, row_start):
        return complex_transposed(
            pick_rows(coupling_one, order_one, shard_piece.shape[0]), shard_piece
        )

    pulled_one = gather_rows(root_solution, fold_mid, jnp.zeros(solved_one.shape, jnp.float32))
    rest_one = solved_one - pulled_one

    def fold_inverse_one(carry, shard_piece, row_start):
        return complex_transposed(inverse_one, shard_piece)

    own_columns = gather_rows(
        rest_one, fold_inverse_one, jnp.zeros((block_rows, width2), jnp.float32)
    )
    mid_block = own_columns + pair_swap(own_columns)
    mid_solution = lax.dynamic_slice_in_dim(mid_block, side * half_rows, half_rows, 0)

    def fold_leaf(carry, shard_piece, row_start):
        return complex_transposed(
            pick_rows(coupling_two, order_two, shard_piece.shape[0]), shard_piece
        )

    pulled_two = gather_rows(mid_block, fold_leaf, jnp.zeros(solved_two.shape, jnp.float32))
    rest_two = solved_two - pulled_two

    def apply_leaf_back(row_start, row_count):
        return complex_transposed(inverse_two, rest_two)

    leaf_solution = scatter_rows(apply_leaf_back, rows_two)
    return (leaf_solution[None], mid_solution[None], root_solution)


def solution(mesh):
    placed = (
        P("leaf", "front", None),
        P("leaf", "front", None),
        P("front", None),
        P("leaf", None, "front", None),
        P("leaf", None, None, "front"),
        P("leaf", None, None, "front"),
        P("leaf", None, None, "front"),
        P(None, "leaf", "front"),
        P("leaf", None),
        P(),
    )
    return jax.shard_map(
        body,
        mesh=mesh,
        in_specs=placed,
        out_specs=(P("leaf", "front", None), P("leaf", "front", None), P("front", None)),
        check_vma=False,
    )
```

profile of v0, /device:TPU:0, one launch (start us, length us, event | category | flops | bytes accessed | tf_op | source)
XLA Modules:
  0.0 1807.4 jit_solution(7411422771738973150)
XLA Ops:
  11.7 6.2 copy.32
  17.8 19.9 %broadcast_clamp_fusion.1 = s32[4096]{0:T(1024)S(1)} fusion(s32[]{:T(128)} %bitcast.35, s32[]{:T(128)} %bitcast.34, s32[]{:T(128)} %bitcast.33, s32[]{:T(128)} %bitcast.32, s32[]{:T(128)} %bitcast.31, s32[]{:T(128)} %bitcast.30, s32[]{:T(128)} %bitcast.29, s32[]{:T(128)} %bitcast.28, s32[]{:T(128)} %bitcast.27, s32[]{:T(128)} %bitcast.26, s32[]{:T(128)} %bitcast.25, ...), kind=kLoop, calls=%fused_computation.211 | loop fusion | flops 356352 | bytes 16512 | tf_op gather
  37.7 30.5 %gather_fusion = f32[4096,2,64]{2,1,0:T(2,128)} fusion(f32[2,4096,64]{2,0,1:T(2,128)} %bitcast.203, s32[4096]{0:T(1024)S(1)} %broadcast_clamp_fusion.1), kind=kCustom, calls=%fused_computation.clone | custom fusion | bytes 4210688 | tf_op jit(solution)/shard_map/jit(_take)/gather | solution.py:45
  68.3 19.9 %compare_and_fusion.1 = pred[4096]{0:T(1024)(128)(4,1)S(1)} fusion(s32[]{:T(128)} %bitcast.35, s32[]{:T(128)} %bitcast.34, s32[]{:T(128)} %bitcast.33, s32[]{:T(128)} %bitcast.32, s32[]{:T(128)} %bitcast.31, s32[]{:T(128)} %bitcast.30, s32[]{:T(128)} %bitcast.29, s32[]{:T(128)} %bitcast.28, s32[]{:T(128)} %bitcast.27, s32[]{:T(128)} %bitcast.26, ...), kind=kLoop, calls=%fused_computation.210 | loop fusion | flops 364544 | bytes 4224 | tf_op jit(solution)/shard_map/jit(_take)/and | solution.py:45
  88.2 16.3 select_bitcast_fusion.1
  104.5 4.1 fusion.158
  108.6 54.6 %all-gather.15.cloned.1.call-done = f32[1,2048,128]{2,1,0:T(8,128)} async-done(((f32[1,64,128]{2,1,0:T(8,128)}), f32[1,2048,128]{2,1,0:T(8,128)}) %all-gather.15.cloned.1.call-update) | async-done | bytes 1048592 | tf_op jit(solution)/shard_map/all_gather | solution.py:49
  179.1 39.6 %compare_and_fusion = (pred[8192]{0:T(1024)(128)(4,1)S(1)}, s32[8192]{0:T(1024)S(1)}) fusion(s32[]{:T(128)} %bitcast.109, s32[]{:T(128)} %bitcast.108, s32[]{:T(128)} %bitcast.107, s32[]{:T(128)} %bitcast.106, s32[]{:T(128)} %bitcast.105, s32[]{:T(128)} %bitcast.104, s32[]{:T(128)} %bitcast.103, s32[]{:T(128)} %bitcast.102, s32[]{:T(128)} %bitcast.101, ...), kind=kLoop, calls=%fused_computation.166 | loop fusion | flops 1253376 | bytes 41216 | tf_op jit(solution)/shard_map/jit(_take)/and | solution.py:45
  218.7 118.7 %reduce-scatter.12.cloned.1.call-done = f32[128,128]{0,1:T(8,128)} async-done(((f32[4096,128]{0,1:T(8,128)}), f32[128,128]{0,1:T(8,128)}) %reduce-scatter.12.cloned.1.call-update) | async-done | bytes 65552 | tf_op jit(solution)/shard_map/reduce_scatter | solution.py:53
  338.5 10.8 copy.34
  349.3 59.6 %gather_fusion.1 = f32[8192,2,64]{2,1,0:T(2,128)} fusion(f32[2,8192,64]{2,0,1:T(2,128)} %bitcast.198, s32[8192]{0:T(1024)S(1)} %broadcast_clamp_fusion), kind=kCustom, calls=%fused_computation.1.clone | custom fusion | bytes 8421376 | tf_op jit(solution)/shard_map/jit(_take)/gather | solution.py:45
  417.3 29.5 %select_bitcast_fusion = f32[2,8192,64]{2,0,1:T(2,128)S(1)} fusion(f32[8192,2,64]{2,1,0:T(2,128)} %gather_fusion.1, pred[8192]{0:T(1024)(128)(4,1)S(1)} %get-tuple-element.20), kind=kLoop, calls=%fused_computation.2 | loop fusion | flops 1048576 | bytes 8396800 | tf_op jit(solution)/shard_map/jit(_take)/select_n | solution.py:45
  446.8 7.7 fusion.157
  454.5 120.2 %reduce-scatter.16.cloned.1.call-done = f32[64,128]{1,0:T(8,128)} async-done(((f32[2048,128]{1,0:T(8,128)}), f32[64,128]{1,0:T(8,128)}) %reduce-scatter.16.cloned.1.call-update) | async-done | bytes 32784
  574.7 6.0 fusion.167
  580.8 4.4 fusion.168
  588.1 165.2 %reduce-scatter.14.cloned.1.call-done = f32[256,128]{0,1:T(8,128)} async-done(((f32[8192,128]{0,1:T(8,128)}), f32[256,128]{0,1:T(8,128)}) %reduce-scatter.14.cloned.1.call-update) | async-done | bytes 131088 | tf_op jit(solution)/shard_map/reduce_scatter | solution.py:53
  753.9 38.4 %all-reduce.3.cloned.1.call-done = f32[256,128]{0,1:T(8,128)} async-done(((f32[256,128]{0,1:T(8,128)}), f32[256,128]{0,1:T(8,128)}) %all-reduce.3.cloned.1.call-update) | async-done | bytes 131088 | tf_op jit(solution)/shard_map/psum | solution.py:66
  792.3 3.9 convolution_bitcast_fusion.5
  796.2 3.9 convolution_bitcast_fusion.4
  803.9 160.8 %reduce-scatter.18.cloned.1.call-done = f32[64,128]{1,0:T(8,128)} async-done(((f32[2048,128]{1,0:T(8,128)}), f32[64,128]{1,0:T(8,128)}) %reduce-scatter.18.cloned.1.call-update) | async-done | bytes 32784 | tf_op jit(solution)/shard_map/reduce_scatter | solution.py:53
  964.8 148.6 %all-gather.7.cloned.1.call-done = f32[2048,128]{1,0:T(8,128)} async-done(((f32[64,128]{1,0:T(8,128)}), f32[2048,128]{1,0:T(8,128)}) %all-gather.7.cloned.1.call-update) | async-done | bytes 1048592 | tf_op jit(solution)/shard_map/all_gather | solution.py:49
  1113.4 3.8 fusion.10
  1117.2 3.8 fusion.13
  1121.7 40.5 %all-reduce.5.cloned.1.call-done = f32[256,128]{0,1:T(8,128)} async-done(((f32[256,128]{0,1:T(8,128)}), f32[256,128]{0,1:T(8,128)}) %all-reduce.5.cloned.1.call-update) | async-done | bytes 131088 | tf_op jit(solution)/shard_map/psum | solution.py:66
  1162.4 158.7 %all-gather.9.cloned.1.call-done = f32[8192,128]{0,1:T(8,128)} async-done(((f32[256,128]{0,1:T(8,128)}), f32[8192,128]{0,1:T(8,128)}) %all-gather.9.cloned.1.call-update) | async-done | bytes 4194320 | tf_op jit(solution)/shard_map/all_gather | solution.py:49
  1321.1 10.3 fusion.169
  1331.5 7.1 fusion.170
  1339.4 150.8 %all-gather.11.cloned.1.call-done = f32[2048,128]{1,0:T(8,128)} async-done(((f32[64,128]{1,0:T(8,128)}), f32[2048,128]{1,0:T(8,128)}) %all-gather.11.cloned.1.call-update) | async-done | bytes 1048592 | tf_op jit(solution)/shard_map/all_gather | solution.py:49
  1499.0 125.6 %all-gather.13.cloned.1.call-done = f32[4096,128]{0,1:T(8,128)} async-done(((f32[128,128]{0,1:T(8,128)}), f32[4096,128]{0,1:T(8,128)}) %all-gather.13.cloned.1.call-update) | async-done | bytes 2097168 | tf_op jit(solution)/shard_map/all_gather | solution.py:49
  1624.6 5.8 fusion.171
  1639.5 159.1 %reduce-scatter.20.cloned.1.call-done = f32[64,128]{1,0:T(8,128)} async-done(((f32[2048,128]{1,0:T(8,128)}), f32[64,128]{1,0:T(8,128)}) %reduce-scatter.20.cloned.1.call-update) | async-done | bytes 32784
  (110 shorter events, 57.9 us)
Async XLA Ops:
  7.2 166.6 %copy-start = (s32[2,64]{1,0:T(2,128)S(1)}, s32[2,64]{1,0:T(2,128)}, u32[]{:S(2)}) copy-start(s32[2,64]{1,0:T(2,128)} %param.27) | copy-start | bytes 1540
  7.2 156.1 %all-gather.15.cloned.1.call-start = ((), (), s32[]{:S(2)}) async-start(), calls=%async_computation.13 | async-start | bytes 1081344 | tf_op jit(solution)/shard_map/all_gather | solution.py:49
  7.9 329.5 %reduce-scatter.12.cloned.1.call-start = ((), (), s32[]{:S(2)}) async-start(), calls=%async_computation.5 | async-start | bytes 2162688 | tf_op jit(solution)/shard_map/reduce_scatter | solution.py:53
  104.5 58.7 %copy-start.7 = (f32[1,2,64,2048]{3,2,1,0:T(8,128)S(1)}, f32[1,2,64,2048]{3,2,1,0:T(8,128)}, u32[]{:S(2)}) copy-start(f32[1,2,64,2048]{3,2,1,0:T(8,128)} %param.21) | copy-start | bytes 3145732
  163.2 4.3 copy-start.4
  172.0 1.6 copy-start.12
  173.6 401.1 %reduce-scatter.16.cloned.1.call-start = ((), (), s32[]{:S(2)}) async-start(), calls=%async_computation.14 | async-start | bytes 1081344
  338.3 70.6 %collective-permute-start = (f32[128,128]{0,1:T(8,128)S(1)}, f32[128,128]{0,1:T(8,128)S(1)}, u32[]{:S(2)}, u32[]{:S(2)}) collective-permute-start(f32[128,128]{0,1:T(8,128)S(1)} %sub.65), channel_id=1, source_target_pairs={{0,32},{32,0},{64,96},{96,64},{1,33},{33,1},{65,97},{97,65},{2,34}... | collective-permute-start | bytes 196616 | tf_op jit(solution)/shard_map/ppermute | solution.py:10
  417.2 336.1 %reduce-scatter.14.cloned.1.call-start = ((), (), s32[]{:S(2)}) async-start(), calls=%async_computation.6 | async-start | bytes 4325376 | tf_op jit(solution)/shard_map/reduce_scatter | solution.py:53
  574.7 6.1 copy-start.2
  574.7 6.1 copy-start.10
  588.0 165.7 %copy-start.11 = (f32[256,128]{1,0:T(8,128)S(1)}, f32[256,128]{1,0:T(8,128)}, u32[]{:S(2)}) copy-start(f32[256,128]{1,0:T(8,128)} %param.20) | copy-start | bytes 393220
  588.0 204.2 %all-reduce.3.cloned.1.call-start = ((), (), s32[]{:S(2)}) async-start(), calls=%async_computation.7 | async-start | bytes 262144 | tf_op jit(solution)/shard_map/psum | solution.py:66
  753.3 211.5 %reduce-scatter.18.cloned.1.call-start = ((), (), s32[]{:S(2)}) async-start(), calls=%async_computation.15 | async-start | bytes 1081344 | tf_op jit(solution)/shard_map/reduce_scatter | solution.py:53
  803.9 309.5 %all-gather.7.cloned.1.call-start = ((), (), s32[]{:S(2)}) async-start(), calls=%async_computation.8 | async-start | bytes 1081344 | tf_op jit(solution)/shard_map/all_gather | solution.py:49
  964.8 197.4 %all-reduce.5.cloned.1.call-start = ((), (), s32[]{:S(2)}) async-start(), calls=%async_computation.9 | async-start | bytes 262144 | tf_op jit(solution)/shard_map/psum | solution.py:66
  1121.7 199.5 %all-gather.9.cloned.1.call-start = ((), (), s32[]{:S(2)}) async-start(), calls=%async_computation.10 | async-start | bytes 4325376 | tf_op jit(solution)/shard_map/all_gather | solution.py:49
  1162.2 328.1 %all-gather.11.cloned.1.call-start = ((), (), s32[]{:S(2)}) async-start(), calls=%async_computation.11 | async-start | bytes 1081344 | tf_op jit(solution)/shard_map/all_gather | solution.py:49
  1321.1 10.3 copy-start.3
  1321.1 10.4 copy-start.5
  1339.4 285.2 %all-gather.13.cloned.1.call-start = ((), (), s32[]{:S(2)}) async-start(), calls=%async_computation.12 | async-start | bytes 2162688 | tf_op jit(solution)/shard_map/all_gather | solution.py:49
  1497.0 1.3 collective-permute-start.1
  1499.0 299.6 %reduce-scatter.20.cloned.1.call-start = ((), (), s32[]{:S(2)}) async-start(), calls=%async_computation.16 | async-start | bytes 1081344
  1624.6 5.8 copy-start.6
  1635.2 165.0 %copy-start.1 = (s32[2,64]{1,0:T(2,128)S(1)}, s32[2,64]{1,0:T(2,128)}, u32[]{:S(2)}) copy-start(s32[2,64]{1,0:T(2,128)} %param.27) | copy-start | bytes 1540
  1636.3 1.6 copy-start.9
  1636.3 2.3 copy-start.8
Sparse Core Ops, SparseCore 0:
  9.7 153.5 all-gather.14
  173.7 163.6 reduce-scatter.11
  417.3 157.3 reduce-scatter.15
  588.2 165.0 reduce-scatter.13
  755.6 36.6 all-reduce.2
  804.0 160.7 reduce-scatter.17
  966.4 146.9 all-gather.6
  1121.8 40.3 all-reduce.4
  1163.9 157.1 all-gather.8
  1339.5 150.7 all-gather.10
  1499.1 125.4 all-gather.12
  1638.0 160.5 reduce-scatter.19
where the time goes:
time: 1820 us; the launch traced here: 1810 us
  waiting for transfers between devices  1440 us (79%)
  other arithmetic  140 us (8%)
  local copies, waits for them, and re-layouts  133 us (7%)
  matrix products  74.3 us (4%)
    all_gather x5, waiting for transfers between devices, gather_rows(): lax.all_gather(local_rows, 'front', axis=0, tiled=True)  638 us
    reduce_scatter x3, waiting for transfers between devices, scatter_rows(): lax.psum_scatter(term(jnp.int32(0), rows_each * lax.axis_size('front')),...  445 us
    unnamed x14, waiting for transfers between devices  280 us
    gather x2, local copies, waits for them, and re-layouts, pick_rows(): return jnp.take(matrix, sources, axis=1)  90.1 us
    psum x2, waiting for transfers between devices, group_total(): return lax.psum(values, 'leaf')  78.9 us
    and x2, other arithmetic, pick_rows(): return jnp.take(matrix, sources, axis=1)  59.5 us
    select_n x2, other arithmetic, pick_rows(): return jnp.take(matrix, sources, axis=1)  45.9 us
  transfers between devices with their start and end apart: 14, of which 13 were waited for; matrix products, arithmetic and copies ran while one was open for 14% of the time, Pallas kernels for 0%

commit v1 on v0

v1 whole, which is shorter than its diff:
```python
import jax
import jax.numpy as jnp
from jax import lax
from jax.experimental import pallas as pl
from jax.experimental.pallas import tpu as pltpu
from jax.sharding import PartitionSpec as P

MESH = pl.DeviceIdType.MESH
F32 = jnp.float32
BF16 = jnp.bfloat16
NF = 32


def halves(x):
    hi = x.astype(BF16)
    lo = (x - hi.astype(F32)).astype(BF16)
    return hi, lo


def packed(x):
    return jnp.concatenate(halves(x), axis=1)


def turn(x):
    swapped = pltpu.roll(x, 64, 1)
    lane = lax.broadcasted_iota(jnp.int32, x.shape, 1)
    return jnp.where(lane < 64, -swapped, swapped)


def stacked(x):
    both = jnp.concatenate([packed(x), packed(turn(x))], axis=0)
    return jnp.concatenate([both, both], axis=0)


def dot(a, b):
    return jnp.dot(a, b, preferred_element_type=F32)


def fold(a):
    return a[:, :128] + a[:, 128:]


def combine(a, n):
    folded = fold(a)
    real = folded[:n] + folded[2 * n : 3 * n]
    imag = folded[n : 2 * n] + folded[3 * n :]
    return real + turn(imag)


def kernel(
    inv_two, inv_one, leaf_src, mid_src, root_src, leaf_inv, leaf_cpl, mid_inv, mid_cpl, root_inv,
    leaf_out, mid_out, root_out,
    st_l, st_c, st_m, st_k, st_r,
    lb, lt, cb, ct, mf, mt, kb, kt, rf, rt,
    ra, rb, rk, gx, gk, send, obuf, xbuf, xred, ybuf, xroot, zbuf, zsum, mx, acc, solved2, solved1,
    ld, ss, rs, xs_s, xs_r, gk_r, gk_fs, gk_fr, gx_r, gx_fs, gx_fr,
):
    leaf = lax.axis_index("leaf")
    me = lax.axis_index("front")
    h = lax.rem(leaf, 2)
    level = lax.div(leaf, 2)
    partner = (leaf + 1 - 2 * h, me)
    across = (lax.rem(leaf + 2, 4), me)

    def rcopy(src, dst, s, r, dev):
        return pltpu.make_async_remote_copy(
            src_ref=src, dst_ref=dst, send_sem=s, recv_sem=r, device_id=dev, device_id_type=MESH
        )

    def load_columns(src, dst, sem):
        def step(b, c):
            cols = pl.ds(pl.multiple_of(b * 128, 128), 128)
            pltpu.make_async_copy(src.at[:, :, cols], dst.at[b], sem).start()
            return c

        lax.fori_loop(0, dst.shape[0], step, 0)

    def loaded(dst, sem):
        pltpu.make_async_copy(dst, dst, sem).wait()

    load_columns(leaf_inv, st_l, ld.at[0])
    load_columns(leaf_cpl, st_c, ld.at[1])
    pltpu.make_async_copy(mid_inv, st_m, ld.at[2]).start()
    load_columns(mid_cpl, st_k, ld.at[3])
    pltpu.make_async_copy(root_inv, st_r, ld.at[4]).start()

    barrier = pltpu.get_barrier_semaphore()

    def greet(d, c):
        pl.semaphore_signal(barrier, 1, device_id=(leaf, lax.rem(me + d, NF)), device_id_type=MESH)
        return c

    lax.fori_loop(1, NF, greet, 0)
    pl.semaphore_signal(barrier, 1, device_id=partner, device_id_type=MESH)
    pl.semaphore_signal(barrier, 1, device_id=across, device_id_type=MESH)
    pl.semaphore_wait(barrier, NF + 1)

    def send_all(src, dst, ph):
        def step(d, c):
            rcopy(src, dst, ss.at[ph], rs.at[ph], (leaf, lax.rem(me + d, NF))).start()
            return c

        lax.fori_loop(1, NF, step, 0)

    def all_sent(buf, ph):
        some = buf.at[pl.ds(0, NF - 1)]
        rcopy(some, some, ss.at[ph], rs.at[ph], partner).wait_send()

    def all_here(buf, ph):
        some = buf.at[pl.ds(0, NF - 1)]
        rcopy(some, some, ss.at[ph], rs.at[ph], partner).wait_recv()

    def split_columns(st, b_ref, t_ref):
        def step(b, c):
            t = st[b].reshape(128, 128)
            hi, lo = halves(t)
            b_ref[b, 0:128, :] = hi
            b_ref[b, 128:256, :] = lo
            hi, lo = halves(t.T)
            t_ref[b, :, 0:128] = hi
            t_ref[b, :, 128:256] = lo
            return c

        lax.fori_loop(0, st.shape[0], step, 0)

    def split_rows(st, f_ref, t_ref, n):
        def step(b, c):
            rows = pl.ds(pl.multiple_of(b * 128, 128), 128)
            for part in range(2):
                t = st[part, rows, :]
                hi, lo = halves(t)
                f_ref[b, :, part * n : (part + 1) * n] = hi
                f_ref[b, :, (2 + part) * n : (3 + part) * n] = lo
                hi, lo = halves(t.T)
                t_ref[b, part * n : (part + 1) * n, :] = hi
                t_ref[b, (2 + part) * n : (3 + part) * n, :] = lo
            return c

        lax.fori_loop(0, 16, step, 0)

    ra[me] = leaf_src[...]
    send_all(leaf_src, ra.at[me], 0)
    loaded(st_l, ld.at[0])
    split_columns(st_l, lb, lt)
    loaded(st_c, ld.at[1])
    split_columns(st_c, cb, ct)
    all_here(ra, 0)
    lhs = jnp.concatenate([lb[b] for b in range(16)], axis=1)
    x = combine(dot(lhs, packed(ra[...].reshape(2048, 128))), 64)
    solved2[...] = x

    def lift(x, t_ref, block_of, o_ref, x_ref, r_ref, per, ph):
        half = o_ref.shape[2]
        groups = NF // per
        rhs = stacked(x)

        def start(g):
            return per * lax.rem(lax.div(me, per) + 1 + g, groups)

        def exchange(g):
            rows = pl.ds(start(g), per)
            return rcopy(o_ref.at[rows, 1 - h], x_ref.at[rows], xs_s.at[g], xs_r.at[g], partner)

        def finish(g):
            exchange(g).wait_recv()
            for i in range(per):
                j = start(g) + i
                o_ref[j, h] = o_ref[j, h] + x_ref[j]

                @pl.when(j != me)
                def _():
                    rcopy(o_ref.at[j, h], r_ref.at[me], ss.at[ph], rs.at[ph], (leaf, j)).start()

                @pl.when(j == me)
                def _():
                    r_ref[j] = o_ref[j, h]

        def step(g, c):
            j = start(g)
            lhs = jnp.concatenate([t_ref[block_of(j, i)] for i in range(4)], axis=0)
            out = fold(dot(lhs, rhs))
            o_ref[pl.ds(j, per)] = out.reshape(per, 2, half, 128)
            exchange(g).start()

            @pl.when(g > 0)
            def _():
                finish(g - 1)

            return c

        lax.fori_loop(0, groups, step, 0)
        finish(groups - 1)

        def done(g, c):
            exchange(g).wait_send()
            return c

        lax.fori_loop(0, groups, done, 0)

    obuf2 = obuf.at[:, :, pl.ds(0, 64)]
    xbuf2 = xbuf.at[:, pl.ds(0, 64)]
    lift(x, ct, lambda j, i: inv_two[0, j + i], obuf2, xbuf2, rb, 4, 1)
    loaded(st_m, ld.at[2])
    split_rows(st_m, mf, mt, 128)
    all_here(rb, 1)
    xred[h] = mid_src[...] - jnp.sum(rb[...], axis=0)
    swap = rcopy(xred.at[h], xred.at[h], ss.at[10], rs.at[10], partner)
    swap.start()
    swap.wait()
    x = xred[...].reshape(128, 128)

    def apply(x, f_ref, r_ref, ph):
        rhs = stacked(x)

        def step(g, c):
            j = 4 * lax.rem(lax.div(me, 4) + 1 + g, 8)
            b = lax.div(j, 2)
            lhs = jnp.concatenate([f_ref[b], f_ref[b + 1]], axis=0)
            send[pl.ds(j, 4)] = fold(dot(lhs, rhs)).reshape(4, 64, 128)
            for i in range(4):

                @pl.when(j + i != me)
                def _():
                    rcopy(send.at[j + i], r_ref.at[me], ss.at[ph], rs.at[ph], (leaf, j + i)).start()

            return c

        lax.fori_loop(0, 8, step, 0)
        r_ref[me] = send[me]

    all_sent(ra, 0)
    apply(x, mf, ra, 2)
    all_sent(rb, 1)
    loaded(st_k, ld.at[3])
    split_columns(st_k, kb, kt)
    all_here(ra, 2)
    x = jnp.sum(ra[...], axis=0)
    solved1[...] = x

    lift(x, kt, lambda j, i: inv_one[level, 2 * j + i], obuf, xbuf, rk, 2, 3)
    loaded(st_r, ld.at[4])
    split_rows(st_r, rf, rt, 256)
    all_here(rk, 3)
    ybuf[0] = jnp.sum(rk[...], axis=0)
    swap = rcopy(ybuf.at[0], ybuf.at[1], ss.at[11], rs.at[11], across)
    swap.start()
    swap.wait()
    rows = pl.ds(pl.multiple_of(h * 128, 128), 128)
    xroot[h] = root_src[rows, :] - (ybuf[0] + ybuf[1])
    swap = rcopy(xroot.at[h], xroot.at[h], ss.at[12], rs.at[12], partner)
    swap.start()
    swap.wait()
    x = xroot[...].reshape(256, 128)

    all_sent(ra, 2)
    apply(x, rf, rb, 4)
    all_here(rb, 4)
    gx1 = gx.at[:, 0]
    gx1[me] = jnp.sum(rb[...], axis=0)
    send_all(gx1.at[me], gx1.at[me], 5)
    all_here(gx1, 5)
    rhs = packed(gx1[...].reshape(2048, 128))

    for m in range(2):
        part = []
        for b in range(16):
            part.append(rt[b, m * 512 : (m + 1) * 512, :])
        acc[m * 512 : (m + 1) * 512, :] = dot(jnp.concatenate(part, axis=1), rhs)
    x = combine(acc[...], 256)
    zbuf[...] = x.reshape(2, 128, 128)
    swap = rcopy(zbuf.at[1 - h], zsum.at[0], ss.at[13], rs.at[13], partner)
    swap.start()
    swap.wait()
    zsum[1] = zbuf[h] + zsum[0]
    swap = rcopy(zsum.at[1], zsum.at[2], ss.at[14], rs.at[14], across)
    swap.start()
    swap.wait()
    gk[me, h] = zsum[1] + zsum[2]

    def gather(g_ref, r, fs, fr, ph, use, groups, per):
        def step(d, c):
            rcopy(g_ref.at[me, h], g_ref.at[me, h], ss.at[ph], r.at[me], (leaf, lax.rem(me + d, NF))).start()
            return c

        lax.fori_loop(1, NF, step, 0)

        def forward(j):
            return rcopy(g_ref.at[j, h], g_ref.at[j, h], fs.at[j], fr.at[j], partner)

        def other(j):
            return rcopy(g_ref.at[j, 1 - h], g_ref.at[j, 1 - h], fs.at[j], fr.at[j], partner)

        def source(g, i):
            return lax.rem(me + NF - (g * per + i), NF)

        def arrive(g):
            for i in range(per):
                j = source(g, i)

                @pl.when(j != me)
                def _():
                    rcopy(g_ref.at[j, h], g_ref.at[j, h], ss.at[ph], r.at[j], partner).wait_recv()

                forward(j).start()

        def consume(g):
            for i in range(per):
                other(source(g, i)).wait_recv()
            use(g, [source(g, i) for i in range(per)])

        def loop(g, c):
            arrive(g)

            @pl.when(g > 0)
            def _():
                consume(g - 1)

            return c

        lax.fori_loop(0, groups, loop, 0)
        consume(groups - 1)

        def done(j, c):
            forward(j).wait_send()
            return c

        lax.fori_loop(0, NF, done, 0)

    acc[0:256, :] = jnp.zeros((256, 256), F32)

    def use_root(g, js):
        lhs = jnp.concatenate([kb[inv_one[level, 2 * j + i]] for j in js for i in range(2)], axis=1)
        rhs = jnp.concatenate([packed(gk[j].reshape(256, 128)) for j in js], axis=0)
        acc[0:256, :] += dot(lhs, rhs)

    gather(gk, gk_r, gk_fs, gk_fr, 6, use_root, 8, 4)
    root_out[...] = gk[me].reshape(256, 128)
    x = solved1[...] - combine(acc[0:256, :], 64)

    ra[me] = x
    send_all(ra.at[me], ra.at[me], 7)
    all_here(ra, 7)
    rhs = packed(ra[...].reshape(2048, 128))
    x = combine(dot(jnp.concatenate([mt[b] for b in range(16)], axis=1), rhs), 128)
    mx[0:2] = x.reshape(2, 64, 128)
    all_sent(gx1, 5)
    swap = rcopy(mx.at[1 - h], mx.at[2], ss.at[15], rs.at[15], partner)
    swap.start()
    swap.wait()
    gx[me, h] = mx[h] + mx[2]
    mid_out[...] = gx[me, h]

    acc[0:256, :] = jnp.zeros((256, 256), F32)

    def use_mid(g, js):
        lhs = jnp.concatenate([cb[inv_two[0, j]] for j in js], axis=1)
        rhs = jnp.concatenate([packed(gx[j].reshape(128, 128)) for j in js], axis=0)
        acc[0:256, :] += dot(lhs, rhs)

    gather(gx, gx_r, gx_fs, gx_fr, 8, use_mid, 4, 8)
    x = solved2[...] - combine(acc[0:256, :], 64)

    all_sent(rb, 4)
    rhs = stacked(x)

    def last(g, c):
        j = 4 * lax.rem(lax.div(me, 4) + 1 + g, 8)
        b = lax.div(j, 2)
        lhs = jnp.concatenate([lt[b], lt[b + 1]], axis=0)
        send[pl.ds(j, 4)] = fold(dot(lhs, rhs)).reshape(4, 64, 128)
        for i in range(4):

            @pl.when(j + i != me)
            def _():
                rcopy(send.at[j + i], rb.at[me], ss.at[9], rs.at[9], (leaf, j + i)).start()

        return c

    lax.fori_loop(0, 8, last, 0)
    rb[me] = send[me]
    all_here(rb, 9)
    leaf_out[...] = jnp.sum(rb[...], axis=0)
    all_sent(rk, 3)
    all_sent(gk.at[:, 0], 6)
    all_sent(ra, 7)
    all_sent(gx1, 8)
    all_sent(rb, 9)


def inverse_order(blocks):
    count = blocks.shape[1]
    ids = jnp.arange(count, dtype=jnp.int32)
    hit = blocks[:, :, None] == ids[None, None, :]
    return jnp.sum(jnp.where(hit, ids[None, :, None], 0), axis=1)


def body(
    leaf_source, mid_source, root_source, leaf_inverse, leaf_coupling, mid_inverse, mid_coupling,
    root_inverse, leaf_blocks, mid_blocks,
):
    vmem = pl.BlockSpec(memory_space=pltpu.VMEM)
    smem = pl.BlockSpec(memory_space=pltpu.SMEM)
    hbm = pl.BlockSpec(memory_space=pl.ANY)
    v = pltpu.VMEM
    dma = pltpu.SemaphoreType.DMA
    leaf_out, mid_out, root_out = pl.pallas_call(
        kernel,
        out_shape=(
            jax.ShapeDtypeStruct((64, 128), F32),
            jax.ShapeDtypeStruct((64, 128), F32),
            jax.ShapeDtypeStruct((256, 128), F32),
        ),
        in_specs=[smem, smem, vmem, vmem, vmem, hbm, hbm, hbm, hbm, hbm],
        out_specs=(vmem, vmem, vmem),
        scratch_shapes=[
            v((16, 2, 64, 128), F32), v((32, 2, 64, 128), F32), v((2, 2048, 128), F32),
            v((64, 2, 64, 128), F32), v((2, 2048, 256), F32),
            v((16, 256, 128), BF16), v((16, 128, 256), BF16),
            v((32, 256, 128), BF16), v((32, 128, 256), BF16),
            v((16, 128, 512), BF16), v((16, 512, 128), BF16),
            v((64, 256, 128), BF16), v((64, 128, 256), BF16),
            v((16, 128, 1024), BF16), v((16, 1024, 128), BF16),
            v((32, 64, 128), F32), v((32, 64, 128), F32), v((32, 128, 128), F32),
            v((32, 2, 64, 128), F32), v((32, 2, 128, 128), F32),
            v((32, 64, 128), F32), v((32, 2, 128, 128), F32), v((32, 128, 128), F32),
            v((2, 64, 128), F32), v((2, 128, 128), F32), v((2, 128, 128), F32),
            v((2, 128, 128), F32), v((3, 128, 128), F32), v((3, 64, 128), F32),
            v((1024, 256), F32), v((64, 128), F32), v((64, 128), F32),
            dma((5,)), dma((16,)), dma((16,)), dma((16,)), dma((16,)),
            dma((32,)), dma((32,)), dma((32,)), dma((32,)), dma((32,)), dma((32,)),
        ],
        compiler_params=pltpu.CompilerParams(
            collective_id=0, has_side_effects=True, vmem_limit_bytes=67043328
        ),
    )(
        inverse_order(leaf_blocks), inverse_order(mid_blocks),
        leaf_source[0], mid_source[0], root_source,
        leaf_inverse[0], jnp.swapaxes(leaf_coupling[0], 1, 2), mid_inverse[0],
        jnp.swapaxes(mid_coupling[0], 1, 2), root_inverse,
    )
    return leaf_out[None], mid_out[None], root_out


def solution(mesh):
    placed = (
        P("leaf", "front", None), P("leaf", "front", None), P("front", None),
        P("leaf", None, "front", None), P("leaf", None, None, "front"),
        P("leaf", None, None, "front"), P("leaf", None, None, "front"),
        P(None, "leaf", "front"), P("leaf", None), P(),
    )
    return jax.shard_map(
        body,
        mesh=mesh,
        in_specs=placed,
        out_specs=(P("leaf", "front", None), P("leaf", "front", None), P("front", None)),
        check_vma=False,
    )
```

time: 1820 us -> 235 us (0.13)
  waiting for transfers between devices: 1440 us -> 0 us
  Pallas kernels: 0 us -> 227 us
  other arithmetic: 140 us -> 2.59 us
  local copies, waits for them, and re-layouts: 133 us -> 4.32 us
  matrix products: 74.3 us -> 0 us
    all_gather x5 -> x0, waiting for transfers between devices: 638 us -> none  [gather_rows(): lax.all_gather(local_rows, 'front', axis=0, tiled=True)]
    reduce_scatter x3 -> x0, waiting for transfers between devices: 445 us -> none  [scatter_rows(): lax.psum_scatter(term(jnp.int32(0), rows_each * lax.axis_size('front')),...]
    unnamed x14 -> x0, waiting for transfers between devices: 280 us -> none
    pallas_call x0 -> x1, Pallas kernels: none -> 227 us  [body(): pl.pallas_call(kernel, out_shape=(jax.ShapeDtypeStruct((64, 128), F32), j...]
    gather x8 -> x0, local copies, waits for them, and re-layouts: 94.4 us -> none  [the longest x2 90.1 us: pick_rows(): return jnp.take(matrix, sources, axis=1)]
    psum x2 -> x0, waiting for transfers between devices: 78.9 us -> none  [group_total(): return lax.psum(values, 'leaf')]
    dot_general x20 -> x0, matrix products: 74.3 us -> none  [the longest x5 24.4 us: complex_transposed(): lax.dot_general(matrix[0], vectors, dims, precision=exact_precision, pref...]
    and x2 -> x0, other arithmetic: 59.5 us -> none  [pick_rows(): return jnp.take(matrix, sources, axis=1)]
  transfers between devices with their start and end apart: 14 -> 0, of which waited for: 13 -> 0; matrix products, arithmetic and copies ran while one was open for 14% -> 0% of each run, Pallas kernels for 0% -> 0%
where the time goes in v1:
time: 235 us
  Pallas kernels  227 us (97%)
  local copies, waits for them, and re-layouts  4.32 us (2%)
  other arithmetic  2.59 us (1%)
    pallas_call x1, Pallas kernels, body(): pl.pallas_call(kernel, out_shape=(jax.ShapeDtypeStruct((64, 128), F32), j...  227 us

profile of v1, /device:TPU:0, one launch (start us, length us, event | category | flops | bytes accessed | tf_op | source)
XLA Modules:
  0.0 234.6 jit_solution(9112320572909859426)
XLA Ops:
  0.6 1.3 select_reduce_fusion.1
  1.9 1.3 select_reduce_fusion.inv_one
  3.2 227.1 %shard_map.124 = (f32[64,128]{1,0:T(8,128)}, f32[64,128]{1,0:T(8,128)}, f32[256,128]{1,0:T(8,128)}) custom-call(s32[1,32]{1,0:T(1,128)} %bitcast.22, s32[2,64]{1,0:T(2,128)} %select_reduce_fusion.inv_one, f32[64,128]{1,0:T(8,128)} %bitcast.18, f32[64,128]{1,0:T(8,128)} %bitcast.19, f32[256,128]{1,0:T(8,128)} %root_src.1, f32[2,64,2048]{2,1,0:T(8,128)} %bitcast.17, ...), custom_call_target="tpu_custom_call" | custom-call | tf_op jit(solution)/shard_map/pallas_call | solution.py:406
  230.3 1.4 copy.16
  231.7 1.4 copy.17
  233.1 1.6 copy.18

commit v2 on v1

v2 whole, which is shorter than its diff:
```python
import jax
import jax.numpy as jnp
from jax import lax
from jax.experimental import pallas as pl
from jax.experimental.pallas import tpu as pltpu
from jax.sharding import PartitionSpec as P

MESH = pl.DeviceIdType.MESH
F32 = jnp.float32
BF16 = jnp.bfloat16
NF = 32


def lanes(x):
    return lax.broadcasted_iota(jnp.int32, x.shape, x.ndim - 1)


def low(x):
    return lanes(x) < 64


def quarter(x):
    return lanes(x) // 32


def pick(x, batch):
    x = pltpu.roll(x, 96, 1) if batch else x
    q = quarter(x)
    upper = jnp.where(q == 2, pltpu.roll(x, 64, 1), pltpu.roll(x, 32, 1))
    return jnp.where(q == 0, x, jnp.where(q == 1, pltpu.roll(x, 96, 1), upper))


def join(a, b):
    q = quarter(a)
    upper = jnp.where(q == 2, pltpu.roll(a, 32, 1), b)
    return jnp.where(q == 0, a, jnp.where(q == 1, pltpu.roll(b, 32, 1), upper))


def squeeze(wide):
    n = wide.shape[0] // 64
    parts = wide.reshape(n, 2, 32, 128)
    first, second = parts[:, 0], parts[:, 1]
    return jnp.where(low(first), first, second).reshape(n * 32, 128)


def spread(packed):
    n = packed.shape[0] // 32
    other = pltpu.roll(packed, 64, 1)
    first = jnp.where(low(packed), packed, other).reshape(n, 32, 128)
    second = jnp.where(low(packed), other, packed).reshape(n, 32, 128)
    return jnp.concatenate([first, second], axis=1).reshape(n * 64, 128)


def halves(x):
    hi = x.astype(BF16)
    lo = (x - hi.astype(F32)).astype(BF16)
    return hi, lo


def pair(wide):
    hi = wide.astype(BF16).astype(F32)
    return jnp.where(low(wide), hi, wide - hi).astype(BF16)


def turn(wide):
    swapped = pltpu.roll(wide, 32, 1)
    return jnp.where(lanes(wide) % 64 < 32, -swapped, swapped)


def stacked(wide):
    both = jnp.concatenate([pair(wide), pair(turn(wide))], axis=0)
    return jnp.concatenate([both, both], axis=0)


def dot(a, b):
    return jnp.dot(a, b, preferred_element_type=F32)


def fold(a):
    return a + pltpu.roll(a, 64, 1)


def combine(a, n):
    folded = fold(a)
    real = folded[:n] + folded[2 * n : 3 * n]
    imag = folded[n : 2 * n] + folded[3 * n :]
    return real + turn(imag)


def kernel(
    inv_two, inv_one, leaf_src, mid_src, root_src, leaf_inv, leaf_cpl, mid_inv, mid_cpl, root_inv,
    leaf_out, mid_out, root_out,
    st_l, st_c, st_m, st_k, st_r,
    lb, lt, cb, ct, mf, mt, kb, kt, rf, rt,
    g1_, g6_, g8_, gk_, gx_, send_, obuf_, xbuf_, in1_, in1k_, part_, in2_, in2k_,
    xred_, ybuf_, xroot_, zbuf_, zsum_, mx_, acc, solved2_, solved1_,
    ld, ss_, rs_, fs_, fr_,
):
    leaf = lax.axis_index("leaf")
    me = lax.axis_index("front")
    h = lax.rem(leaf, 2)
    level = lax.div(leaf, 2)
    partner = (leaf + 1 - 2 * h, me)
    across = (lax.rem(leaf + 2, 4), me)
    my_x = lax.rem(me, 4)
    my_z = lax.rem(lax.div(me, 4), 4)
    my_y = lax.div(me, 16)
    line = (my_z, my_x)
    spot = (my_y * 4 + my_x, my_y * 4 + my_z)

    def on_line(way, i):
        return (leaf, my_y * 16 + (i * 4 + my_x if way == 0 else my_z * 4 + i))

    def in_plane(way, u):
        y, other = lax.div(u, 4), lax.rem(u, 4)
        return (leaf, y * 16 + (my_z * 4 + other if way == 0 else other * 4 + my_x))

    def along(way, d):
        return lax.rem(line[way] + d, 4)

    def around(way, d):
        return lax.rem(spot[way] + d, 8)

    def rcopy(src, dst, s, r, dev):
        return pltpu.make_async_remote_copy(
            src_ref=src, dst_ref=dst, send_sem=s, recv_sem=r, device_id=dev, device_id_type=MESH
        )

    def load_columns(src, dst, sem):
        def step(b, c):
            cols = pl.ds(pl.multiple_of(b * 128, 128), 128)
            pltpu.make_async_copy(src.at[:, :, cols], dst.at[b], sem).start()
            return c

        lax.fori_loop(0, dst.shape[0], step, 0)

    def loaded(dst, sem):
        pltpu.make_async_copy(dst, dst, sem).wait()

    load_columns(leaf_inv, st_l, ld.at[0])
    load_columns(leaf_cpl, st_c, ld.at[1])
    pltpu.make_async_copy(mid_inv, st_m, ld.at[2]).start()
    load_columns(mid_cpl, st_k, ld.at[3])
    pltpu.make_async_copy(root_inv, st_r, ld.at[4]).start()

    barrier = pltpu.get_barrier_semaphore()

    def greet(dev):
        pl.semaphore_signal(barrier, 1, device_id=dev, device_id_type=MESH)

    for d in range(1, 8):
        greet(in_plane(0, around(0, d)))
        if d != 4:
            greet(in_plane(1, around(1, d)))
    greet(partner)
    greet(across)
    pl.semaphore_wait(barrier, 15)

    def split_columns(st, b_ref, t_ref):
        def step(b, c):
            t = st[b].reshape(128, 128)
            hi, lo = halves(t)
            b_ref[b, 0:128, :] = hi
            b_ref[b, 128:256, :] = lo
            hi, lo = halves(t.T)
            t_ref[b, :, 0:128] = hi
            t_ref[b, :, 128:256] = lo
            return c

        lax.fori_loop(0, st.shape[0], step, 0)

    def split_rows(st, f_ref, t_ref, n):
        def step(b, c):
            rows = pl.ds(pl.multiple_of(b * 128, 128), 128)
            for part in range(2):
                t = st[part, rows, :]
                hi, lo = halves(t)
                f_ref[b, :, part * n : (part + 1) * n] = hi
                f_ref[b, :, (2 + part) * n : (3 + part) * n] = lo
                hi, lo = halves(t.T)
                t_ref[b, part * n : (part + 1) * n, :] = hi
                t_ref[b, (2 + part) * n : (3 + part) * n, :] = lo
            return c

        lax.fori_loop(0, 16, step, 0)

    def chain(batch):
        g1, g6, g8, gk, gx = (r.at[batch] for r in (g1_, g6_, g8_, gk_, gx_))
        send, obuf, xbuf, in1, in1k = (r.at[batch] for r in (send_, obuf_, xbuf_, in1_, in1k_))
        part, xred, ybuf, xroot = (r.at[batch] for r in (part_, xred_, ybuf_, xroot_))
        zbuf, zsum, mx, in2k = (r.at[batch] for r in (zbuf_, zsum_, mx_, in2k_))
        solved2, solved1 = solved2_.at[batch], solved1_.at[batch]
        ss, rs, fs, fr = (r.at[batch] for r in (ss_, rs_, fs_, fr_))
        part16 = part.at[:, :, pl.ds(0, 16)]

        def wait_send(some, k):
            rcopy(some, some, ss.at[k], rs.at[k], partner).wait_send()

        def wait_recv(some, k):
            rcopy(some, some, ss.at[k], rs.at[k], partner).wait_recv()

        def three(buf, way):
            return buf.at[way, pl.ds(0, 3)]

        def seven(buf, way):
            return buf.at[way, pl.ds(0, 7)]

        def sum_send(way, d, out, into, k):
            to = along(way, d)
            rcopy(
                out.at[way, to], into.at[way, line[way]], ss.at[k + way], rs.at[k + way], on_line(way, to)
            ).start()

        def sum_own(out, into):
            for way in range(2):
                into[way, line[way]] = out[way, line[way]]

        def sum_second(into, part, into2, k):
            for way in range(2):
                wait_recv(three(into, way), k + way)
            for way in range(2):
                part[way] = jnp.sum(into[way], axis=0)
                into2[way, spot[way]] = part[way, spot[way]]
            for way in range(2):
                for d in range(1, 8):
                    u = around(way, d)
                    rcopy(
                        part.at[way, u], into2.at[way, spot[way]], ss.at[k + 2 + way], rs.at[k + 2 + way],
                        in_plane(way, u),
                    ).start()

        def sum_last(into2, k):
            for way in range(2):
                wait_recv(seven(into2, way), k + 2 + way)
            return jnp.concatenate([jnp.sum(into2[0], axis=0), jnp.sum(into2[1], axis=0)], axis=0)

        def sum_sent(into, into2, k):
            for way in range(2):
                wait_send(three(into, way), k + way)
                wait_send(seven(into2, way), k + 2 + way)

        def share_first(rows, g, k):
            n = rows.shape[0] // 2
            for way in range(2):
                g[way, line[way], spot[way]] = rows[way * n : (way + 1) * n]
                mine = g.at[way, line[way], spot[way]]
                for d in range(1, 8):
                    u = around(way, d)
                    rcopy(mine, mine, ss.at[k + way], rs.at[k + way], in_plane(way, u)).start()

        def share_second(g, k):
            for way in range(2):
                wait_recv(g.at[way, 0, pl.ds(0, 7)], k + way)
                mine = g.at[way, line[way]]
                for d in range(1, 4):
                    to = on_line(way, along(way, d))
                    rcopy(mine, mine, ss.at[k + 2 + way], rs.at[k + 2 + way], to).start()

        def share_last(g, k):
            for way in range(2):
                wait_recv(three(g, way), k + 2 + way)

        def share_sent(g, k):
            for way in range(2):
                wait_send(g.at[way, 0, pl.ds(0, 7)], k + way)
                wait_send(three(g, way), k + 2 + way)

        def rows_of(g):
            rows = []
            for j in range(NF):
                y, z, x = j // 16, j // 4 % 4, j % 4
                rows += [g[0, z, y * 4 + x], g[1, x, y * 4 + z]]
            return pair(spread(jnp.concatenate(rows, axis=0)))

        def lift_exchange(o_ref, x_ref, way, i, k):
            at = 4 * way + i
            return rcopy(o_ref.at[1 - h, way, i], x_ref.at[way, i], fs.at[k + at], fr.at[k + at], partner)

        def lift_start(x, t_ref, blocks_of, o_ref, x_ref, subs, k):
            rhs = stacked(x)
            n = o_ref.shape[4]
            wide = 8 // subs

            def step(d, c):
                z = along(0, d)

                def sub(s, c):
                    u = s * wide
                    y, x0 = lax.div(u, 4), lax.rem(u, 4)
                    j = y * 16 + z * 4 + x0
                    lhs = jnp.concatenate([t_ref[b] for b in blocks_of(j)], axis=0)
                    out = squeeze(fold(dot(lhs, rhs))).reshape(wide, 2, 2 * n, 128)
                    for i in range(wide):
                        for side in range(2):
                            o_ref[side, 0, z, u + i] = out[i, side, 0:n]
                            o_ref[side, 1, x0 + i, y * 4 + z] = out[i, side, n : 2 * n]
                    return c

                lax.fori_loop(0, subs, sub, 0)
                lift_exchange(o_ref, x_ref, 0, z, k).start()
                return c

            lax.fori_loop(1, 5, step, 0)
            for d in range(1, 5):
                lift_exchange(o_ref, x_ref, 1, along(1, d), k).start()

        def lift_send(o_ref, x_ref, into, k, phase):
            mine = o_ref.at[h]
            for way in range(2):
                for d in range(1, 5):
                    i = along(way, d)
                    lift_exchange(o_ref, x_ref, way, i, k).wait_recv()
                    mine[way, i] = mine[way, i] + x_ref[way, i]
                    if d < 4:
                        sum_send(way, d, mine, into, phase)
            sum_own(mine, into)
            for way in range(2):
                for i in range(4):
                    lift_exchange(o_ref, x_ref, way, i, k).wait_send()

        def apply(x, f_ref, into, phase):
            rhs = stacked(x)

            def step(d, c):
                z = along(0, d)
                lhs = jnp.concatenate([f_ref[8 * y + 2 * z + i] for y in range(2) for i in range(2)], axis=0)
                out = squeeze(fold(dot(lhs, rhs))).reshape(8, 32, 128)
                send[0, z] = out[:, 0:16]
                for u in range(8):
                    send[1, u % 4, u // 4 * 4 + z] = out[u, 16:32]

                @pl.when(d < 4)
                def _():
                    sum_send(0, d, send, into, phase)

                return c

            lax.fori_loop(1, 5, step, 0)
            for d in range(1, 4):
                sum_send(1, d, send, into, phase)
            sum_own(send, into)

        def forward(g_ref, side, way, i, k):
            at = k + 4 * way + i
            return rcopy(g_ref.at[side, way, i], g_ref.at[side, way, i], fs.at[at], fr.at[at], partner)

        def forward_own(g_ref, k):
            for way in range(2):
                forward(g_ref, h, way, line[way], k).start()

        def forward_rest(g_ref, k):
            for way in range(2):
                for d in range(1, 4):
                    forward(g_ref, h, way, along(way, d), k).start()

        def gather_use(g_ref, blocks_of, b_ref, k):
            for way in range(2):
                for i in range(4):
                    forward(g_ref, 1 - h, way, i, k).wait_recv()
            acc[0:256, :] = jnp.zeros((256, 128), F32)

            def step(z, c):
                lhs, rows = [], []
                for u in range(8):
                    y, x = u // 4, u % 4
                    lhs += [b_ref[b] for b in blocks_of(y * 16 + z * 4 + x)]
                    for side in range(2):
                        rows += [g_ref[side, 0, z, u], g_ref[side, 1, x, y * 4 + z]]
                rhs = pair(spread(jnp.concatenate(rows, axis=0)))
                acc[0:256, :] += dot(jnp.concatenate(lhs, axis=1), rhs)
                return c

            lax.fori_loop(0, 4, step, 0)
            for way in range(2):
                for i in range(4):
                    forward(g_ref, h, way, i, k).wait_send()
            return combine(acc[0:256, :], 64)

        def swap(src, dst, k, dev):
            copy = rcopy(src, dst, ss.at[k], rs.at[k], dev)
            copy.start()
            return copy

        share_first(squeeze(pick(leaf_src[...], batch)), g1, 0)
        yield
        share_second(g1, 0)
        yield
        share_last(g1, 0)
        lhs = jnp.concatenate([lb[b] for b in range(16)], axis=1)
        x = combine(dot(lhs, rows_of(g1)), 64)
        solved2[...] = x
        obuf2 = obuf.at[:, :, :, :, pl.ds(0, 16)]
        xbuf2 = xbuf.at[:, :, :, pl.ds(0, 16)]
        in2 = in2_.at[batch, 0]
        lift_start(x, ct, lambda j: [inv_two[0, j + i] for i in range(4)], obuf2, xbuf2, 2, 0)
        yield
        lift_send(obuf2, xbuf2, in1, 0, 4)
        yield
        sum_second(in1, part16, in2, 4)
        yield
        xred[h] = squeeze(pick(mid_src[...], batch)) - sum_last(in2, 4)
        copy = swap(xred.at[h], xred.at[h], 40, partner)
        yield
        copy.wait()
        in2 = in2_.at[batch, 1]
        apply(spread(xred[...].reshape(64, 128)), mf, in1, 8)
        yield
        sum_sent(in1, in2, 4)
        sum_second(in1, part16, in2, 8)
        yield
        x = spread(sum_last(in2, 8))
        solved1[...] = x
        lift_start(
            x, kt, lambda j: [inv_one[level, 2 * j + i] for i in range(4)], obuf, xbuf, 4, 8
        )
        yield
        lift_send(obuf, xbuf, in1k, 8, 12)
        yield
        sum_sent(in1, in2, 8)
        sum_second(in1k, part, in2k, 12)
        yield
        ybuf[0] = sum_last(in2k, 12)
        copy = swap(ybuf.at[0], ybuf.at[1], 41, across)
        yield
        copy.wait()
        rows = pl.ds(pl.multiple_of(h * 128, 128), 128)
        xroot[h] = squeeze(pick(root_src[rows, :], batch)) - (ybuf[0] + ybuf[1])
        copy = swap(xroot.at[h], xroot.at[h], 42, partner)
        yield
        copy.wait()
        in2 = in2_.at[batch, 2]
        apply(spread(xroot[...].reshape(128, 128)), rf, in1, 16)
        yield
        sum_sent(in1k, in2k, 12)
        sum_second(in1, part16, in2, 16)
        yield
        share_first(sum_last(in2, 16), g6, 20)
        yield
        share_second(g6, 20)
        yield
        share_last(g6, 20)
        rhs = rows_of(g6)
        for m in range(2):
            lhs = jnp.concatenate([rt[b, m * 512 : (m + 1) * 512, :] for b in range(16)], axis=1)
            acc[m * 512 : (m + 1) * 512, :] = dot(lhs, rhs)
        zbuf[...] = squeeze(combine(acc[...], 256)).reshape(2, 64, 128)
        copy = swap(zbuf.at[1 - h], zsum.at[0], 43, partner)
        yield
        copy.wait()
        zsum[1] = zbuf[h] + zsum[0]
        copy = swap(zsum.at[1], zsum.at[2], 44, across)
        yield
        copy.wait()
        share_first(zsum[1] + zsum[2], gk.at[h], 24)
        yield
        share_second(gk.at[h], 24)
        forward_own(gk, 16)
        yield
        share_last(gk.at[h], 24)
        forward_rest(gk, 16)
        yield
        pulled = gather_use(gk, lambda j: [inv_one[level, 2 * j], inv_one[level, 2 * j + 1]], kb, 16)
        share_first(squeeze(solved1[...] - pulled), g8, 28)
        yield
        share_second(g8, 28)
        yield
        share_last(g8, 28)
        lhs = jnp.concatenate([mt[b] for b in range(16)], axis=1)
        x = combine(dot(lhs, rows_of(g8)), 128)
        mx[0:2] = squeeze(x).reshape(2, 32, 128)
        copy = swap(mx.at[1 - h], mx.at[2], 45, partner)
        yield
        copy.wait()
        share_first(mx[h] + mx[2], gx.at[h], 32)
        yield
        share_second(gx.at[h], 32)
        forward_own(gx, 24)
        yield
        share_last(gx.at[h], 32)
        forward_rest(gx, 24)
        yield
        pulled = gather_use(gx, lambda j: [inv_two[0, j]], cb, 24)
        sum_sent(in1, in2, 16)
        in2 = in2_.at[batch, 3]
        apply(solved2[...] - pulled, lt, in1, 36)
        yield
        sum_second(in1, part16, in2, 36)
        yield
        solved2[...] = spread(sum_last(in2, 36))
        sum_sent(in1, in2, 36)
        share_sent(g1, 0)
        share_sent(g6, 20)
        share_sent(gk.at[h], 24)
        share_sent(g8, 28)
        share_sent(gx.at[h], 32)

    def prepare_leaf():
        loaded(st_l, ld.at[0])
        split_columns(st_l, lb, lt)
        loaded(st_c, ld.at[1])
        split_columns(st_c, cb, ct)

    def prepare_mid():
        loaded(st_m, ld.at[2])
        split_rows(st_m, mf, mt, 128)

    def prepare_mid_coupling():
        loaded(st_k, ld.at[3])
        split_columns(st_k, kb, kt)

    def prepare_root():
        loaded(st_r, ld.at[4])
        split_rows(st_r, rf, rt, 256)

    prepare = {0: prepare_leaf, 1: prepare_mid, 3: prepare_mid_coupling, 6: prepare_root}
    batches = [chain(0), chain(1)]
    running, at = True, 0
    while running:
        for solve in batches:
            running = next(solve, True) is None
        prepare.get(at, lambda: None)()
        at += 1
    leaf_out[...] = join(solved2_[0], solved2_[1])

    def own_rows(g):
        halves_of = []
        for side in range(2):
            halves_of += [g[side, way, line[way], spot[way]] for way in range(2)]
        return halves_of

    mid = [spread(jnp.concatenate([gx_[b, h, w, line[w], spot[w]] for w in range(2)], axis=0)) for b in range(2)]
    mid_out[...] = join(*mid)
    root_out[...] = join(*[spread(jnp.concatenate(own_rows(gk_.at[b]), axis=0)) for b in range(2)])


def inverse_order(blocks):
    count = blocks.shape[1]
    ids = jnp.arange(count, dtype=jnp.int32)
    hit = blocks[:, :, None] == ids[None, None, :]
    return jnp.sum(jnp.where(hit, ids[None, :, None], 0), axis=1)


def body(
    leaf_source, mid_source, root_source, leaf_inverse, leaf_coupling, mid_inverse, mid_coupling,
    root_inverse, leaf_blocks, mid_blocks,
):
    vmem = pl.BlockSpec(memory_space=pltpu.VMEM)
    smem = pl.BlockSpec(memory_space=pltpu.SMEM)
    hbm = pl.BlockSpec(memory_space=pl.ANY)
    v = pltpu.VMEM
    dma = pltpu.SemaphoreType.DMA
    leaf_out, mid_out, root_out = pl.pallas_call(
        kernel,
        out_shape=(
            jax.ShapeDtypeStruct((64, 128), F32),
            jax.ShapeDtypeStruct((64, 128), F32),
            jax.ShapeDtypeStruct((256, 128), F32),
        ),
        in_specs=[smem, smem, vmem, vmem, vmem, hbm, hbm, hbm, hbm, hbm],
        out_specs=(vmem, vmem, vmem),
        scratch_shapes=[
            v((16, 2, 64, 128), F32), v((32, 2, 64, 128), F32), v((2, 2048, 128), F32),
            v((64, 2, 64, 128), F32), v((2, 2048, 256), F32),
            v((16, 256, 128), BF16), v((16, 128, 256), BF16),
            v((32, 256, 128), BF16), v((32, 128, 256), BF16),
            v((16, 128, 512), BF16), v((16, 512, 128), BF16),
            v((64, 256, 128), BF16), v((64, 128, 256), BF16),
            v((16, 128, 1024), BF16), v((16, 1024, 128), BF16),
            v((2, 2, 4, 8, 16, 128), F32), v((2, 2, 4, 8, 16, 128), F32), v((2, 2, 4, 8, 16, 128), F32),
            v((2, 2, 2, 4, 8, 32, 128), F32), v((2, 2, 2, 4, 8, 16, 128), F32),
            v((2, 2, 4, 8, 16, 128), F32), v((2, 2, 2, 4, 8, 32, 128), F32), v((2, 2, 4, 8, 32, 128), F32),
            v((2, 2, 4, 8, 16, 128), F32), v((2, 2, 4, 8, 32, 128), F32), v((2, 2, 8, 32, 128), F32),
            v((2, 4, 2, 8, 16, 128), F32), v((2, 2, 8, 32, 128), F32),
            v((2, 2, 32, 128), F32), v((2, 2, 64, 128), F32), v((2, 2, 64, 128), F32),
            v((2, 2, 64, 128), F32), v((2, 3, 64, 128), F32), v((2, 3, 32, 128), F32),
            v((1024, 128), F32), v((2, 64, 128), F32), v((2, 64, 128), F32),
            dma((5,)), dma((2, 48)), dma((2, 48)), dma((2, 32)), dma((2, 32)),
        ],
        compiler_params=pltpu.CompilerParams(
            collective_id=0, has_side_effects=True, vmem_limit_bytes=67043328
        ),
    )(
        inverse_order(leaf_blocks), inverse_order(mid_blocks),
        leaf_source[0], mid_source[0], root_source,
        leaf_inverse[0], jnp.swapaxes(leaf_coupling[0], 1, 2), mid_inverse[0],
        jnp.swapaxes(mid_coupling[0], 1, 2), root_inverse,
    )
    return leaf_out[None], mid_out[None], root_out


def solution(mesh):
    placed = (
        P("leaf", "front", None), P("leaf", "front", None), P("front", None),
        P("leaf", None, "front", None), P("leaf", None, None, "front"),
        P("leaf", None, None, "front"), P("leaf", None, None, "front"),
        P(None, "leaf", "front"), P("leaf", None), P(),
    )
    return jax.shard_map(
        body,
        mesh=mesh,
        in_specs=placed,
        out_specs=(P("leaf", "front", None), P("leaf", "front", None), P("front", None)),
        check_vma=False,
    )
```

time: 235 us -> 187 us (0.80)
  Pallas kernels: 227 us -> 180 us
    pallas_call x1, Pallas kernels: 227 us -> 180 us  [body(): pl.pallas_call(kernel, out_shape=(jax.ShapeDtypeStruct((64, 128), F32), j...]
where the time goes in v2:
time: 187 us
  Pallas kernels  180 us (96%)
  local copies, waits for them, and re-layouts  4.32 us (2%)
  other arithmetic  2.59 us (1%)
    pallas_call x1, Pallas kernels, body(): pl.pallas_call(kernel, out_shape=(jax.ShapeDtypeStruct((64, 128), F32), j...  180 us
    unnamed x3, local copies, waits for them, and re-layouts  4.32 us

profile of v2, /device:TPU:0, one launch (start us, length us, event | category | flops | bytes accessed | tf_op | source)
XLA Modules:
  0.0 187.2 jit_solution(12213931148468780115)
XLA Ops:
  0.6 1.3 select_reduce_fusion.1
  1.9 1.3 select_reduce_fusion.inv_one
  3.2 179.6 %shard_map.124 = (f32[64,128]{1,0:T(8,128)}, f32[64,128]{1,0:T(8,128)}, f32[256,128]{1,0:T(8,128)}) custom-call(s32[1,32]{1,0:T(1,128)} %bitcast.22, s32[2,64]{1,0:T(2,128)} %select_reduce_fusion.inv_one, f32[64,128]{1,0:T(8,128)} %bitcast.18, f32[64,128]{1,0:T(8,128)} %bitcast.19, f32[256,128]{1,0:T(8,128)} %root_src.1, f32[2,64,2048]{2,1,0:T(8,128)} %bitcast.17, ...), custom_call_target="tpu_custom_call" | custom-call | tf_op jit(solution)/shard_map/pallas_call | solution.py:552
  182.9 1.4 copy.16
  184.2 1.4 copy.17
  185.6 1.6 copy.18

commit v3 on v2

--- a/solution.py
+++ b/solution.py
@@ -93,7 +93,7 @@
     st_l, st_c, st_m, st_k, st_r,
     lb, lt, cb, ct, mf, mt, kb, kt, rf, rt,
     g1_, g6_, g8_, gk_, gx_, send_, obuf_, xbuf_, in1_, in1k_, part_, in2_, in2k_,
-    xred_, ybuf_, xroot_, zbuf_, zsum_, mx_, acc, solved2_, solved1_,
+    xred_, xroot_, zbuf_, zsum_, mx_, acc, solved2_, solved1_,
     ld, ss_, rs_, fs_, fr_,
 ):
     leaf = lax.axis_index("leaf")
@@ -148,26 +148,31 @@
     def greet(dev):
         pl.semaphore_signal(barrier, 1, device_id=dev, device_id_type=MESH)
 
-    for d in range(1, 8):
-        greet(in_plane(0, around(0, d)))
-        if d != 4:
-            greet(in_plane(1, around(1, d)))
+    for d in range(8):
+        for way in range(2):
+            if d % 4 or way == 0:
+                dev = in_plane(way, around(way, d))
+                greet((across[0], dev[1]))
+                if d:
+                    greet(dev)
     greet(partner)
-    greet(across)
-    pl.semaphore_wait(barrier, 15)
+    greet((across[0] + partner[0] - leaf, me))
+    pl.semaphore_wait(barrier, 29)
 
     def split_columns(st, b_ref, t_ref):
-        def step(b, c):
-            t = st[b].reshape(128, 128)
-            hi, lo = halves(t)
-            b_ref[b, 0:128, :] = hi
-            b_ref[b, 128:256, :] = lo
-            hi, lo = halves(t.T)
-            t_ref[b, :, 0:128] = hi
-            t_ref[b, :, 128:256] = lo
+        def step(q, c):
+            for i in range(4):
+                b = 4 * q + i
+                t = st[b].reshape(128, 128)
+                hi, lo = halves(t)
+                b_ref[b, 0:128, :] = hi
+                b_ref[b, 128:256, :] = lo
+                hi, lo = halves(t.T)
+                t_ref[b, :, 0:128] = hi
+                t_ref[b, :, 128:256] = lo
             return c
 
-        lax.fori_loop(0, st.shape[0], step, 0)
+        lax.fori_loop(0, st.shape[0] // 4, step, 0)
 
     def split_rows(st, f_ref, t_ref, n):
         def step(b, c):
@@ -187,7 +192,7 @@
     def chain(batch):
         g1, g6, g8, gk, gx = (r.at[batch] for r in (g1_, g6_, g8_, gk_, gx_))
         send, obuf, xbuf, in1, in1k = (r.at[batch] for r in (send_, obuf_, xbuf_, in1_, in1k_))
-        part, xred, ybuf, xroot = (r.at[batch] for r in (part_, xred_, ybuf_, xroot_))
+        part, xred, xroot = (r.at[batch] for r in (part_, xred_, xroot_))
         zbuf, zsum, mx, in2k = (r.at[batch] for r in (zbuf_, zsum_, mx_, in2k_))
         solved2, solved1 = solved2_.at[batch], solved1_.at[batch]
         ss, rs, fs, fr = (r.at[batch] for r in (ss_, rs_, fs_, fr_))
@@ -202,8 +207,8 @@
         def three(buf, way):
             return buf.at[way, pl.ds(0, 3)]
 
-        def seven(buf, way):
-            return buf.at[way, pl.ds(0, 7)]
+        def all_but_one(buf, way):
+            return buf.at[way, pl.ds(0, buf.shape[1] - 1)]
 
         def sum_send(way, d, out, into, k):
             to = along(way, d)
@@ -215,29 +220,33 @@
             for way in range(2):
                 into[way, line[way]] = out[way, line[way]]
 
-        def sum_second(into, part, into2, k):
+        def sum_second(into, part, into2, k, both=False):
             for way in range(2):
                 wait_recv(three(into, way), k + way)
+            at = [8 * level + spot[way] if both else spot[way] for way in range(2)]
             for way in range(2):
                 part[way] = jnp.sum(into[way], axis=0)
-                into2[way, spot[way]] = part[way, spot[way]]
-            for way in range(2):
+                into2[way, at[way]] = part[way, spot[way]]
+            for way in range(2):
+                slot = into2.at[way, at[way]]
+                sems = ss.at[k + 2 + way], rs.at[k + 2 + way]
+                if both:
+                    for d in range(8):
+                        u = around(way, d)
+                        rcopy(part.at[way, u], slot, *sems, (across[0], in_plane(way, u)[1])).start()
                 for d in range(1, 8):
                     u = around(way, d)
-                    rcopy(
-                        part.at[way, u], into2.at[way, spot[way]], ss.at[k + 2 + way], rs.at[k + 2 + way],
-                        in_plane(way, u),
-                    ).start()
+                    rcopy(part.at[way, u], slot, *sems, in_plane(way, u)).start()
 
         def sum_last(into2, k):
             for way in range(2):
-                wait_recv(seven(into2, way), k + 2 + way)
+                wait_recv(all_but_one(into2, way), k + 2 + way)
             return jnp.concatenate([jnp.sum(into2[0], axis=0), jnp.sum(into2[1], axis=0)], axis=0)
 
         def sum_sent(into, into2, k):
             for way in range(2):
                 wait_send(three(into, way), k + way)
-                wait_send(seven(into2, way), k + 2 + way)
+                wait_send(all_but_one(into2, way), k + 2 + way)
 
         def share_first(rows, g, k):
             n = rows.shape[0] // 2
@@ -276,10 +285,20 @@
             at = 4 * way + i
             return rcopy(o_ref.at[1 - h, way, i], x_ref.at[way, i], fs.at[k + at], fr.at[k + at], partner)
 
-        def lift_start(x, t_ref, blocks_of, o_ref, x_ref, subs, k):
+        def lift(x, t_ref, blocks_of, o_ref, x_ref, subs, k, into, phase):
             rhs = stacked(x)
             n = o_ref.shape[4]
             wide = 8 // subs
+            mine = o_ref.at[h]
+
+            def finish(way, d):
+                i = along(way, d)
+                lift_exchange(o_ref, x_ref, way, i, k).wait_recv()
+                mine[way, i] = mine[way, i] + x_ref[way, i]
+
+                @pl.when(d < 4)
+                def _():
+                    sum_send(way, d, mine, into, phase)
 
             def step(d, c):
                 z = along(0, d)
@@ -298,21 +317,27 @@
 
                 lax.fori_loop(0, subs, sub, 0)
                 lift_exchange(o_ref, x_ref, 0, z, k).start()
+
+                @pl.when(d > 1)
+                def _():
+                    finish(0, d - 1)
+
                 return c
 
             lax.fori_loop(1, 5, step, 0)
-            for d in range(1, 5):
+
+            def second(d, c):
                 lift_exchange(o_ref, x_ref, 1, along(1, d), k).start()
-
-        def lift_send(o_ref, x_ref, into, k, phase):
-            mine = o_ref.at[h]
-            for way in range(2):
-                for d in range(1, 5):
-                    i = along(way, d)
-                    lift_exchange(o_ref, x_ref, way, i, k).wait_recv()
-                    mine[way, i] = mine[way, i] + x_ref[way, i]
-                    if d < 4:
-                        sum_send(way, d, mine, into, phase)
+                return c
+
+            lax.fori_loop(1, 5, second, 0)
+            finish(0, 4)
+
+            def third(d, c):
+                finish(1, d)
+                return c
+
+            lax.fori_loop(1, 5, third, 0)
             sum_own(mine, into)
             for way in range(2):
                 for i in range(4):
@@ -392,15 +417,12 @@
         obuf2 = obuf.at[:, :, :, :, pl.ds(0, 16)]
         xbuf2 = xbuf.at[:, :, :, pl.ds(0, 16)]
         in2 = in2_.at[batch, 0]
-        lift_start(x, ct, lambda j: [inv_two[0, j + i] for i in range(4)], obuf2, xbuf2, 2, 0)
-        yield
-        lift_send(obuf2, xbuf2, in1, 0, 4)
+        lift(x, ct, lambda j: [inv_two[0, j + i] for i in range(4)], obuf2, xbuf2, 2, 0, in1, 4)
         yield
         sum_second(in1, part16, in2, 4)
         yield
         xred[h] = squeeze(pick(mid_src[...], batch)) - sum_last(in2, 4)
         copy = swap(xred.at[h], xred.at[h], 40, partner)
-        yield
         copy.wait()
         in2 = in2_.at[batch, 1]
         apply(spread(xred[...].reshape(64, 128)), mf, in1, 8)
@@ -410,23 +432,16 @@
         yield
         x = spread(sum_last(in2, 8))
         solved1[...] = x
-        lift_start(
-            x, kt, lambda j: [inv_one[level, 2 * j + i] for i in range(4)], obuf, xbuf, 4, 8
+        lift(
+            x, kt, lambda j: [inv_one[level, 2 * j + i] for i in range(4)], obuf, xbuf, 4, 8, in1k, 12
         )
         yield
-        lift_send(obuf, xbuf, in1k, 8, 12)
-        yield
         sum_sent(in1, in2, 8)
-        sum_second(in1k, part, in2k, 12)
-        yield
-        ybuf[0] = sum_last(in2k, 12)
-        copy = swap(ybuf.at[0], ybuf.at[1], 41, across)
-        yield
-        copy.wait()
+        sum_second(in1k, part, in2k, 12, both=True)
+        yield
         rows = pl.ds(pl.multiple_of(h * 128, 128), 128)
-        xroot[h] = squeeze(pick(root_src[rows, :], batch)) - (ybuf[0] + ybuf[1])
+        xroot[h] = squeeze(pick(root_src[rows, :], batch)) - sum_last(in2k, 12)
         copy = swap(xroot.at[h], xroot.at[h], 42, partner)
-        yield
         copy.wait()
         in2 = in2_.at[batch, 2]
         apply(spread(xroot[...].reshape(128, 128)), rf, in1, 16)
@@ -444,21 +459,18 @@
             lhs = jnp.concatenate([rt[b, m * 512 : (m + 1) * 512, :] for b in range(16)], axis=1)
             acc[m * 512 : (m + 1) * 512, :] = dot(lhs, rhs)
         zbuf[...] = squeeze(combine(acc[...], 256)).reshape(2, 64, 128)
-        copy = swap(zbuf.at[1 - h], zsum.at[0], 43, partner)
-        yield
-        copy.wait()
-        zsum[1] = zbuf[h] + zsum[0]
-        copy = swap(zsum.at[1], zsum.at[2], 44, across)
-        yield
-        copy.wait()
-        share_first(zsum[1] + zsum[2], gk.at[h], 24)
+        zsum[leaf] = zbuf[h]
+        for side, dev in ((1 - h, partner), (h, across), (1 - h, (across[0] + partner[0] - leaf, me))):
+            rcopy(zbuf.at[side], zsum.at[leaf], ss.at[43], rs.at[43], dev).start()
+        yield
+        wait_recv(zsum.at[pl.ds(0, 3)], 43)
+        share_first(jnp.sum(zsum[...], axis=0), gk.at[h], 24)
         yield
         share_second(gk.at[h], 24)
         forward_own(gk, 16)
         yield
         share_last(gk.at[h], 24)
         forward_rest(gk, 16)
-        yield
         pulled = gather_use(gk, lambda j: [inv_one[level, 2 * j], inv_one[level, 2 * j + 1]], kb, 16)
         share_first(squeeze(solved1[...] - pulled), g8, 28)
         yield
@@ -469,7 +481,6 @@
         x = combine(dot(lhs, rows_of(g8)), 128)
         mx[0:2] = squeeze(x).reshape(2, 32, 128)
         copy = swap(mx.at[1 - h], mx.at[2], 45, partner)
-        yield
         copy.wait()
         share_first(mx[h] + mx[2], gx.at[h], 32)
         yield
@@ -478,7 +489,6 @@
         yield
         share_last(gx.at[h], 32)
         forward_rest(gx, 24)
-        yield
         pulled = gather_use(gx, lambda j: [inv_two[0, j]], cb, 24)
         sum_sent(in1, in2, 16)
         in2 = in2_.at[batch, 3]
@@ -488,6 +498,7 @@
         yield
         solved2[...] = spread(sum_last(in2, 36))
         sum_sent(in1, in2, 36)
+        wait_send(zsum.at[pl.ds(0, 3)], 43)
         share_sent(g1, 0)
         share_sent(g6, 20)
         share_sent(gk.at[h], 24)
@@ -512,7 +523,7 @@
         loaded(st_r, ld.at[4])
         split_rows(st_r, rf, rt, 256)
 
-    prepare = {0: prepare_leaf, 1: prepare_mid, 3: prepare_mid_coupling, 6: prepare_root}
+    prepare = {0: prepare_leaf, 1: prepare_mid, 2: prepare_mid_coupling, 5: prepare_root}
     batches = [chain(0), chain(1)]
     running, at = True, 0
     while running:
@@ -570,9 +581,9 @@
             v((2, 2, 2, 4, 8, 32, 128), F32), v((2, 2, 2, 4, 8, 16, 128), F32),
             v((2, 2, 4, 8, 16, 128), F32), v((2, 2, 2, 4, 8, 32, 128), F32), v((2, 2, 4, 8, 32, 128), F32),
             v((2, 2, 4, 8, 16, 128), F32), v((2, 2, 4, 8, 32, 128), F32), v((2, 2, 8, 32, 128), F32),
-            v((2, 4, 2, 8, 16, 128), F32), v((2, 2, 8, 32, 128), F32),
-            v((2, 2, 32, 128), F32), v((2, 2, 64, 128), F32), v((2, 2, 64, 128), F32),
-            v((2, 2, 64, 128), F32), v((2, 3, 64, 128), F32), v((2, 3, 32, 128), F32),
+            v((2, 4, 2, 8, 16, 128), F32), v((2, 2, 16, 32, 128), F32),
+            v((2, 2, 32, 128), F32), v((2, 2, 64, 128), F32),
+            v((2, 2, 64, 128), F32), v((2, 4, 64, 128), F32), v((2, 3, 32, 128), F32),
             v((1024, 128), F32), v((2, 64, 128), F32), v((2, 64, 128), F32),
             dma((5,)), dma((2, 48)), dma((2, 48)), dma((2, 32)), dma((2, 32)),
         ],

time: 187 us -> 182 us (0.973)
  Pallas kernels: 180 us -> 174 us
    pallas_call x1, Pallas kernels: 180 us -> 174 us  [body(): pl.pallas_call(kernel, out_shape=(jax.ShapeDtypeStruct((64, 128), F32), j...]
where the time goes in v3:
time: 182 us
  Pallas kernels  174 us (96%)
  local copies, waits for them, and re-layouts  4.32 us (2%)
  other arithmetic  2.59 us (1%)
    pallas_call x1, Pallas kernels, body(): pl.pallas_call(kernel, out_shape=(jax.ShapeDtypeStruct((64, 128), F32), j...  174 us
    unnamed x3, local copies, waits for them, and re-layouts  4.32 us

profile of v3, /device:TPU:0, one launch (start us, length us, event | category | flops | bytes accessed | tf_op | source)
XLA Modules:
  0.0 181.7 jit_solution(2521477685027479198)
XLA Ops:
  0.6 1.3 select_reduce_fusion.1
  1.9 1.3 select_reduce_fusion.inv_one
  3.2 174.2 %shard_map.124 = (f32[64,128]{1,0:T(8,128)}, f32[64,128]{1,0:T(8,128)}, f32[256,128]{1,0:T(8,128)}) custom-call(s32[1,32]{1,0:T(1,128)} %bitcast.22, s32[2,64]{1,0:T(2,128)} %select_reduce_fusion.inv_one, f32[64,128]{1,0:T(8,128)} %bitcast.18, f32[64,128]{1,0:T(8,128)} %bitcast.19, f32[256,128]{1,0:T(8,128)} %root_src.1, f32[2,64,2048]{2,1,0:T(8,128)} %bitcast.17, ...), custom_call_target="tpu_custom_call" | custom-call | tf_op jit(solution)/shard_map/pallas_call | solution.py:563
  177.4 1.4 copy.16
  178.8 1.4 copy.17
  180.1 1.6 copy.18

commit v4 on v3

--- a/solution.py
+++ b/solution.py
@@ -88,7 +88,7 @@
 
 
 def kernel(
-    inv_two, inv_one, leaf_src, mid_src, root_src, leaf_inv, leaf_cpl, mid_inv, mid_cpl, root_inv,
+    orders, leaf_src, mid_src, root_src, leaf_inv, leaf_cpl, mid_inv, mid_cpl, root_inv,
     leaf_out, mid_out, root_out,
     st_l, st_c, st_m, st_k, st_r,
     lb, lt, cb, ct, mf, mt, kb, kt, rf, rt,
@@ -137,12 +137,6 @@
     def loaded(dst, sem):
         pltpu.make_async_copy(dst, dst, sem).wait()
 
-    load_columns(leaf_inv, st_l, ld.at[0])
-    load_columns(leaf_cpl, st_c, ld.at[1])
-    pltpu.make_async_copy(mid_inv, st_m, ld.at[2]).start()
-    load_columns(mid_cpl, st_k, ld.at[3])
-    pltpu.make_async_copy(root_inv, st_r, ld.at[4]).start()
-
     barrier = pltpu.get_barrier_semaphore()
 
     def greet(dev):
@@ -157,6 +151,8 @@
                     greet(dev)
     greet(partner)
     greet((across[0] + partner[0] - leaf, me))
+    load_columns(leaf_inv, st_l, ld.at[0])
+    load_columns(leaf_cpl, st_c, ld.at[1])
     pl.semaphore_wait(barrier, 29)
 
     def split_columns(st, b_ref, t_ref):
@@ -417,7 +413,7 @@
         obuf2 = obuf.at[:, :, :, :, pl.ds(0, 16)]
         xbuf2 = xbuf.at[:, :, :, pl.ds(0, 16)]
         in2 = in2_.at[batch, 0]
-        lift(x, ct, lambda j: [inv_two[0, j + i] for i in range(4)], obuf2, xbuf2, 2, 0, in1, 4)
+        lift(x, ct, lambda j: [orders[2, j + i] for i in range(4)], obuf2, xbuf2, 2, 0, in1, 4)
         yield
         sum_second(in1, part16, in2, 4)
         yield
@@ -433,7 +429,7 @@
         x = spread(sum_last(in2, 8))
         solved1[...] = x
         lift(
-            x, kt, lambda j: [inv_one[level, 2 * j + i] for i in range(4)], obuf, xbuf, 4, 8, in1k, 12
+            x, kt, lambda j: [orders[level, 2 * j + i] for i in range(4)], obuf, xbuf, 4, 8, in1k, 12
         )
         yield
         sum_sent(in1, in2, 8)
@@ -471,7 +467,7 @@
         yield
         share_last(gk.at[h], 24)
         forward_rest(gk, 16)
-        pulled = gather_use(gk, lambda j: [inv_one[level, 2 * j], inv_one[level, 2 * j + 1]], kb, 16)
+        pulled = gather_use(gk, lambda j: [orders[level, 2 * j], orders[level, 2 * j + 1]], kb, 16)
         share_first(squeeze(solved1[...] - pulled), g8, 28)
         yield
         share_second(g8, 28)
@@ -489,7 +485,7 @@
         yield
         share_last(gx.at[h], 32)
         forward_rest(gx, 24)
-        pulled = gather_use(gx, lambda j: [inv_two[0, j]], cb, 24)
+        pulled = gather_use(gx, lambda j: [orders[2, j]], cb, 24)
         sum_sent(in1, in2, 16)
         in2 = in2_.at[batch, 3]
         apply(solved2[...] - pulled, lt, in1, 36)
@@ -506,6 +502,9 @@
         share_sent(gx.at[h], 32)
 
     def prepare_leaf():
+        pltpu.make_async_copy(mid_inv, st_m, ld.at[2]).start()
+        load_columns(mid_cpl, st_k, ld.at[3])
+        pltpu.make_async_copy(root_inv, st_r, ld.at[4]).start()
         loaded(st_l, ld.at[0])
         split_columns(st_l, lb, lt)
         loaded(st_c, ld.at[1])
@@ -549,6 +548,12 @@
     ids = jnp.arange(count, dtype=jnp.int32)
     hit = blocks[:, :, None] == ids[None, None, :]
     return jnp.sum(jnp.where(hit, ids[None, :, None], 0), axis=1)
+
+
+def hand_over(leaf_in, mid_in, root_in, leaf_out, mid_out, root_out):
+    leaf_out[...] = leaf_in[...]
+    mid_out[...] = mid_in[...]
+    root_out[...] = root_in[...]
 
 
 def body(
@@ -567,7 +572,7 @@
             jax.ShapeDtypeStruct((64, 128), F32),
             jax.ShapeDtypeStruct((256, 128), F32),
         ),
-        in_specs=[smem, smem, vmem, vmem, vmem, hbm, hbm, hbm, hbm, hbm],
+        in_specs=[smem, vmem, vmem, vmem, hbm, hbm, hbm, hbm, hbm],
         out_specs=(vmem, vmem, vmem),
         scratch_shapes=[
             v((16, 2, 64, 128), F32), v((32, 2, 64, 128), F32), v((2, 2048, 128), F32),
@@ -591,11 +596,21 @@
             collective_id=0, has_side_effects=True, vmem_limit_bytes=67043328
         ),
     )(
-        inverse_order(leaf_blocks), inverse_order(mid_blocks),
+        inverse_order(jnp.concatenate([mid_blocks, jnp.pad(leaf_blocks, ((0, 0), (0, 32)), constant_values=-1)])),
         leaf_source[0], mid_source[0], root_source,
         leaf_inverse[0], jnp.swapaxes(leaf_coupling[0], 1, 2), mid_inverse[0],
         jnp.swapaxes(mid_coupling[0], 1, 2), root_inverse,
     )
+    leaf_out, mid_out, root_out = pl.pallas_call(
+        hand_over,
+        out_shape=(
+            jax.ShapeDtypeStruct((64, 128), F32),
+            jax.ShapeDtypeStruct((64, 128), F32),
+            jax.ShapeDtypeStruct((256, 128), F32),
+        ),
+        in_specs=[vmem, vmem, vmem],
+        out_specs=(vmem, vmem, vmem),
+    )(leaf_out, mid_out, root_out)
     return leaf_out[None], mid_out[None], root_out
 
 

time: 182 us -> 177 us (0.973)
  local copies, waits for them, and re-layouts: 4.32 us -> 0 us
    unnamed x3 -> x0, local copies, waits for them, and re-layouts: 4.32 us -> none
    reduce_sum x2 -> x1, other arithmetic: 2.59 us -> 0.69 us  [inverse_order(): return jnp.sum(jnp.where(hit, ids[None, :, None], 0), axis=1)]
where the time goes in v4:
time: 177 us
  Pallas kernels  175 us (99%)
    pallas_call x1, Pallas kernels, body(): pl.pallas_call(kernel, out_shape=(jax.ShapeDtypeStruct((64, 128), F32), j...  173 us

profile of v4, /device:TPU:0, one launch (start us, length us, event | category | flops | bytes accessed | tf_op | source)
XLA Modules:
  0.0 176.9 jit_solution(12374957303711234433)
XLA Ops:
  0.6 0.7 select_add_fusion
  1.3 0.7 select_reduce_fusion.orders
  2.0 173.2 %shard_map.121 = (f32[64,128]{1,0:T(8,128)}, f32[64,128]{1,0:T(8,128)}, f32[256,128]{1,0:T(8,128)}) custom-call(s32[3,64]{1,0:T(4,128)} %select_reduce_fusion.orders, f32[64,128]{1,0:T(8,128)} %bitcast.16, f32[64,128]{1,0:T(8,128)} %bitcast.17, f32[256,128]{1,0:T(8,128)} %root_src.1, f32[2,64,2048]{2,1,0:T(8,128)} %bitcast.15, f32[2,64,4096]{2,1,0:T(8,128)} %bitcast.13, ...), custom_call_target="tpu_custom_call" | custom-call | tf_op jit(solution)/shard_map/pallas_call | solution.py:568
  175.3 1.6 shard_map.122
